TPU v7x, 32 devices: a whole 2x2x4 slice. The times are simulated.
32 devices in a mesh: node: 8 (over z, x), rep: 4 (over y, core).
Axes of the slice: x: 2, y: 2, z: 4, core: 2. Of those that a mesh axis runs over, the one named last changes fastest.
Arguments:
- features: bfloat16 [8192, 512], P(('node', 'rep')), may hold values from -6 to 6
- weight: bfloat16 [512, 512], replicated, may hold values from -0.25 to 0.25
- cotangent: bfloat16 [8192, 512], P(('node', 'rep')), may hold values from -6 to 6
- tile_values: bfloat16 [8192, 128, 128], P(('node', 'rep')), may hold values from -0.125 to 0.125
- tile_row: int32 [8192], P(('node', 'rep')), may hold values from 0 to 7
- tile_col: int32 [8192], P(('node', 'rep')), may hold values from 0 to 15
- tile_count: int32 [32], P(('node', 'rep')), may hold values from 64 to 256, as said below
Outputs:
- activation: bfloat16 [8192, 512], P(('node', 'rep'))
- weight_grad: float32 [512, 512], replicated
- feature_grad: bfloat16 [8192, 512], P(('node', 'rep'))
Inputs may be any that keep to these rules, and one draw needn't show every extreme that they name: `tile_count`: slots of a device below its count hold tiles, the others are ignored; some device uses all 256 slots.
All inputs are finite; a program needn't handle non-finite values.
Results may differ from a plain program's by a relative error of at most 0.023.
Values may be sent and summed in bfloat16 or wider, within the bound.
A program may use at most 128 MiB of HBM per device.

v0:
```python
import math
import jax
import jax.numpy as jnp
from jax import lax
from jax.sharding import PartitionSpec as P

TB = 128


def smooth_gate(values):
    return jax.nn.gelu(values, approximate=True)


def apply_tiles(
    tile_values, tile_row, tile_col, tile_count, sources, target_shape, backward, window_start
):
    group_size = min(32, tile_row.shape[0])
    filled = tile_count[0]
    turns_needed = (filled + group_size - 1) // group_size
    window_blocks = target_shape[0]

    def one_turn(turn_index, totals):
        offset = turn_index * group_size
        values = lax.dynamic_slice_in_dim(tile_values, offset, group_size, 0)
        rows_here = lax.dynamic_slice_in_dim(tile_row, offset, group_size, 0)
        cols_here = lax.dynamic_slice_in_dim(tile_col, offset, group_size, 0)
        slot_mask = (offset + jnp.arange(group_size, dtype=jnp.int32) < filled).astype(jnp.float32)
        if backward:
            local_cols = cols_here - window_start
            inside = ((local_cols >= 0) & (local_cols < window_blocks)).astype(jnp.float32)
            placed = jnp.clip(local_cols, 0, window_blocks - 1)
            product = jnp.einsum(
                "tji,tjf->tif", values, sources[rows_here], preferred_element_type=jnp.float32
            )
            return totals.at[placed].add(product * (slot_mask * inside)[:, None, None])
        product = jnp.einsum(
            "tij,tjf->tif", values, sources[cols_here], preferred_element_type=jnp.float32
        )
        return totals.at[rows_here].add(product * slot_mask[:, None, None])

    return lax.fori_loop(0, turns_needed, one_turn, jnp.zeros(target_shape, jnp.float32))


def local(features, weight, cotangent, tile_values, tile_row, tile_col, tile_count):
    rows_quarter = features.shape[0]
    feature_width = features.shape[1]
    rep_count = lax.axis_size("rep")
    node_count = lax.axis_size("node")
    scale = 1.0 / math.sqrt(rows_quarter * rep_count * node_count)
    gathered = lax.all_gather(features, "node", axis=0, tiled=True)
    source_blocks = gathered.reshape(-1, TB, feature_width)
    block_count = rows_quarter * rep_count // TB
    partial_value = apply_tiles(
        tile_values,
        tile_row,
        tile_col,
        tile_count,
        source_blocks,
        (block_count, TB, feature_width),
        False,
        0,
    ).reshape(block_count * TB, feature_width)
    aggregate_all = lax.psum(partial_value, "rep").astype(jnp.bfloat16)
    cotangent_all = lax.all_gather(cotangent, "rep", axis=0, tiled=True)
    pre = jnp.dot(aggregate_all, weight, preferred_element_type=jnp.float32)
    activated, pullback = jax.vjp(smooth_gate, pre)
    grad_all = pullback(cotangent_all.astype(jnp.float32))[0].astype(jnp.bfloat16)
    full_grad = jnp.dot(grad_all, weight.T, preferred_element_type=jnp.float32).astype(jnp.bfloat16)
    offset = lax.axis_index("rep") * rows_quarter
    own_aggregate = lax.dynamic_slice_in_dim(aggregate_all, offset, rows_quarter, 0)
    own_grad = lax.dynamic_slice_in_dim(grad_all, offset, rows_quarter, 0)
    weight_term = jnp.dot(own_aggregate.T, own_grad, preferred_element_type=jnp.float32)
    output_rows = lax.dynamic_slice_in_dim(activated, offset, rows_quarter, 0).astype(jnp.bfloat16)
    weight_grad = lax.psum(weight_term, ("node", "rep")) * scale
    grad_blocks = full_grad.reshape(block_count, TB, feature_width)
    contributions = apply_tiles(
        tile_values, tile_row, tile_col, tile_count, grad_blocks, source_blocks.shape, True, 0
    )
    feature_grad = lax.psum_scatter(
        contributions.reshape(-1, feature_width).astype(jnp.bfloat16),
        "node",
        scatter_dimension=0,
        tiled=True,
    )
    return (output_rows, weight_grad, feature_grad)


def solution(mesh):
    in_specs = (
        P(("node", "rep"), None),
        P(),
        P(("node", "rep"), None),
        P(("node", "rep"), None, None),
        P(("node", "rep")),
        P(("node", "rep")),
        P(("node", "rep")),
    )
    out_specs = (P(("node", "rep"), None), P(), P(("node", "rep"), None))
    return jax.shard_map(local, mesh=mesh, in_specs=in_specs, out_specs=out_specs, check_vma=False)
```

profile of v0, /device:TPU:0, one launch (start us, length us, event | category | flops | bytes accessed | tf_op | source)
XLA Modules:
  0.0 611.5 jit_solution(17007301135434615890)
XLA Ops:
  7.2 0.0 copy-start
  7.2 0.0 copy-start.1
  7.2 0.0 all-gather.3.cloned.1.call-start
  7.2 0.7 all-gather.3.cloned.1.call-update
  7.9 0.0 all-gather.5.cloned.1.call-start
  8.0 0.7 all-gather.5.cloned.1.call-update
  8.7 0.0 all-reduce.3.cloned.1.call-start
  9.4 52.6 %all-gather.3.cloned.1.call-done = bf16[2048,512]{1,0:T(8,128)(2,1)} async-done(((bf16[256,512]{1,0:T(8,128)(2,1)}), bf16[2048,512]{1,0:T(8,128)(2,1)}) %all-gather.3.cloned.1.call-update) | async-done | bytes 2097168 | tf_op jit(solution)/shard_map/all_gather | solution.py:50
  62.0 0.2 broadcast_in_dim.20
  62.3 95.9 %while.20 = (s32[]{:T(128)}, f32[8,128,512]{2,1,0:T(8,128)S(1)}, s32[]{:T(128)}, s32[256]{0:T(256)S(1)}, bf16[256,128,128]{2,1,0:T(8,128)(2,1)}, /*index=5*/s32[...) while((s32[]{:T(128)}, f32[8,128,512]{2,1,0:T(8,128)S(1)}, ...), condition=%wide.region_2.3_spmd, body=%wide.region_0.2_spmd.sunk | while | flops 541066560 | bytes 47191344 | solution.py:41
  62.3 0.7 compare_convert_fusion.3
  62.9 0.1 compare_select_fusion.6
  63.0 4.4 gather_fusion
  67.4 7.2 %broadcast_multiply_fusion.5 = f32[32,128,512]{2,1,0:T(8,128)} fusion(f32[32]{0:T(128)S(1)} %compare_convert_fusion.3, bf16[32,128,512]{2,1,0:T(8,128)(2,1)} %gather_fusion, bf16[256,128,128]{2,1,0:T(8,128)(2,1)} %get-tuple-element.274, s32[]{:T(128)S(6)} %select_n.44), kind=kOutput, calls=%fused_computation.4.clone.1 | convolution fusion | flops 538968064 | bytes 13631620 | tf_op jit(solution)/shard_map/while/body/tij,tjf->tif/dot_general | solution.py:36
  74.6 11.8 %scatter_fusion = f32[8,128,512]{2,1,0:T(8,128)S(1)} fusion(f32[8,128,512]{2,1,0:T(8,128)S(1)} %get-tuple-element.259, s32[32]{0:T(128)S(1)} %get-tuple-element.234, f32[32,128,512]{2,1,0:T(8,128)} %broadcast_multiply_fusion.5), kind=kCustom, calls=%fused_computation.2.clone.1 | custom fusion | flops 2097152 | bytes 25165952 | tf_op jit(solution)/shard_map/while/body/scatter-add | solution.py:39
  86.4 0.7 compare_convert_fusion.3
  87.1 0.1 compare_select_fusion.6
  87.2 4.4 gather_fusion
  91.5 7.0 %broadcast_multiply_fusion.5 = f32[32,128,512]{2,1,0:T(8,128)} fusion(f32[32]{0:T(128)S(1)} %compare_convert_fusion.3, bf16[32,128,512]{2,1,0:T(8,128)(2,1)} %gather_fusion, bf16[256,128,128]{2,1,0:T(8,128)(2,1)} %get-tuple-element.274, s32[]{:T(128)S(6)} %select_n.44), kind=kOutput, calls=%fused_computation.4.clone.1 | convolution fusion | flops 538968064 | bytes 13631620 | tf_op jit(solution)/shard_map/while/body/tij,tjf->tif/dot_general | solution.py:36
  98.5 11.8 %scatter_fusion = f32[8,128,512]{2,1,0:T(8,128)S(1)} fusion(f32[8,128,512]{2,1,0:T(8,128)S(1)} %get-tuple-element.259, s32[32]{0:T(128)S(1)} %get-tuple-element.234, f32[32,128,512]{2,1,0:T(8,128)} %broadcast_multiply_fusion.5), kind=kCustom, calls=%fused_computation.2.clone.1 | custom fusion | flops 2097152 | bytes 25165952 | tf_op jit(solution)/shard_map/while/body/scatter-add | solution.py:39
  110.3 0.7 compare_convert_fusion.3
  111.0 0.1 compare_select_fusion.6
  111.1 4.4 gather_fusion
  115.4 7.0 %broadcast_multiply_fusion.5 = f32[32,128,512]{2,1,0:T(8,128)} fusion(f32[32]{0:T(128)S(1)} %compare_convert_fusion.3, bf16[32,128,512]{2,1,0:T(8,128)(2,1)} %gather_fusion, bf16[256,128,128]{2,1,0:T(8,128)(2,1)} %get-tuple-element.274, s32[]{:T(128)S(6)} %select_n.44), kind=kOutput, calls=%fused_computation.4.clone.1 | convolution fusion | flops 538968064 | bytes 13631620 | tf_op jit(solution)/shard_map/while/body/tij,tjf->tif/dot_general | solution.py:36
  122.4 11.7 %scatter_fusion = f32[8,128,512]{2,1,0:T(8,128)S(1)} fusion(f32[8,128,512]{2,1,0:T(8,128)S(1)} %get-tuple-element.259, s32[32]{0:T(128)S(1)} %get-tuple-element.234, f32[32,128,512]{2,1,0:T(8,128)} %broadcast_multiply_fusion.5), kind=kCustom, calls=%fused_computation.2.clone.1 | custom fusion | flops 2097152 | bytes 25165952 | tf_op jit(solution)/shard_map/while/body/scatter-add | solution.py:39
  134.2 0.7 compare_convert_fusion.3
  134.8 0.1 compare_select_fusion.6
  134.9 4.4 gather_fusion
  139.3 7.0 %broadcast_multiply_fusion.5 = f32[32,128,512]{2,1,0:T(8,128)} fusion(f32[32]{0:T(128)S(1)} %compare_convert_fusion.3, bf16[32,128,512]{2,1,0:T(8,128)(2,1)} %gather_fusion, bf16[256,128,128]{2,1,0:T(8,128)(2,1)} %get-tuple-element.274, s32[]{:T(128)S(6)} %select_n.44), kind=kOutput, calls=%fused_computation.4.clone.1 | convolution fusion | flops 538968064 | bytes 13631620 | tf_op jit(solution)/shard_map/while/body/tij,tjf->tif/dot_general | solution.py:36
  146.3 11.8 %scatter_fusion = f32[8,128,512]{2,1,0:T(8,128)S(1)} fusion(f32[8,128,512]{2,1,0:T(8,128)S(1)} %get-tuple-element.259, s32[32]{0:T(128)S(1)} %get-tuple-element.234, f32[32,128,512]{2,1,0:T(8,128)} %broadcast_multiply_fusion.5), kind=kCustom, calls=%fused_computation.2.clone.1 | custom fusion | flops 2097152 | bytes 25165952 | tf_op jit(solution)/shard_map/while/body/scatter-add | solution.py:39
  158.1 87.7 %all-reduce.4 = bf16[1024,512]{1,0:T(8,128)(2,1)} all-reduce(f32[1024,512]{1,0:T(8,128)S(1)} %bitcast.16), channel_id=1, replica_groups=mesh['node'=8,'rep'=4] {'rep'}, use_global_device_ids=true, to_apply=%region_3.4 | all-reduce | flops 524288 | bytes 3145728 | tf_op jit(solution)/shard_map/psum | solution.py:63
  245.8 5.3 fusion.6
  251.2 0.7 convolution_convert_fusion
  251.9 2.3 fusion.15
  254.2 0.0 all-reduce.3.cloned.1.call-update
  254.2 0.0 reduce-scatter.2.cloned.1.call-start
  254.3 2.5 broadcast_in_dim.21
  256.8 117.3 %while.21 = (s32[]{:T(128)}, f32[16,128,512]{2,1,0:T(8,128)}, s32[]{:T(128)}, s32[256]{0:T(256)S(1)}, bf16[256,128,128]{2,1,0:T(8,128)(2,1)}, /*index=5*/s32[256...) while((s32[]{:T(128)}, f32[16,128,512]{2,1,0:T(8,128)}, ...), condition=%wide.region_7.8_spmd, body=%wide.region_5.7_spmd.sunk | while | flops 541066688 | bytes 47191480 | solution.py:41
  256.8 0.7 and_select_fusion.2
  257.5 0.1 compare_select_fusion.7
  257.6 2.8 gather_fusion.1
  260.3 7.3 %broadcast_multiply_fusion.6 = f32[32,128,512]{2,1,0:T(8,128)} fusion(f32[32]{0:T(128)S(1)} %and_select_fusion.2, bf16[32,128,512]{2,1,0:T(8,128)(2,1)} %gather_fusion.1, bf16[256,128,128]{2,1,0:T(8,128)(2,1)} %get-tuple-element.310, s32[]{:T(128)S(6)} %select_n.46), kind=kOutput, calls=%fused_computation.11.clone.1 | convolution fusion | flops 538968064 | bytes 13631620 | tf_op jit(solution)/shard_map/while/body/tji,tjf->tif/dot_general | solution.py:32
  267.6 18.4 %scatter_fusion.1 = f32[16,128,512]{2,1,0:T(8,128)} fusion(f32[16,128,512]{2,1,0:T(8,128)} %get-tuple-element.295, s32[32]{0:T(128)S(1)} %get-tuple-element.244, f32[32,128,512]{2,1,0:T(8,128)} %broadcast_multiply_fusion.6), kind=kCustom, calls=%fused_computation.3.clone.1 | custom fusion | flops 2097152 | bytes 25165952 | tf_op jit(solution)/shard_map/while/body/scatter-add | solution.py:35
  286.0 0.7 and_select_fusion.2
  286.7 0.1 compare_select_fusion.7
  286.8 2.8 gather_fusion.1
  289.5 7.3 %broadcast_multiply_fusion.6 = f32[32,128,512]{2,1,0:T(8,128)} fusion(f32[32]{0:T(128)S(1)} %and_select_fusion.2, bf16[32,128,512]{2,1,0:T(8,128)(2,1)} %gather_fusion.1, bf16[256,128,128]{2,1,0:T(8,128)(2,1)} %get-tuple-element.310, s32[]{:T(128)S(6)} %select_n.46), kind=kOutput, calls=%fused_computation.11.clone.1 | convolution fusion | flops 538968064 | bytes 13631620 | tf_op jit(solution)/shard_map/while/body/tji,tjf->tif/dot_general | solution.py:32
  296.8 18.7 %scatter_fusion.1 = f32[16,128,512]{2,1,0:T(8,128)} fusion(f32[16,128,512]{2,1,0:T(8,128)} %get-tuple-element.295, s32[32]{0:T(128)S(1)} %get-tuple-element.244, f32[32,128,512]{2,1,0:T(8,128)} %broadcast_multiply_fusion.6), kind=kCustom, calls=%fused_computation.3.clone.1 | custom fusion | flops 2097152 | bytes 25165952 | tf_op jit(solution)/shard_map/while/body/scatter-add | solution.py:35
  315.5 0.7 and_select_fusion.2
  316.2 0.1 compare_select_fusion.7
  316.3 2.8 gather_fusion.1
  319.0 7.3 %broadcast_multiply_fusion.6 = f32[32,128,512]{2,1,0:T(8,128)} fusion(f32[32]{0:T(128)S(1)} %and_select_fusion.2, bf16[32,128,512]{2,1,0:T(8,128)(2,1)} %gather_fusion.1, bf16[256,128,128]{2,1,0:T(8,128)(2,1)} %get-tuple-element.310, s32[]{:T(128)S(6)} %select_n.46), kind=kOutput, calls=%fused_computation.11.clone.1 | convolution fusion | flops 538968064 | bytes 13631620 | tf_op jit(solution)/shard_map/while/body/tji,tjf->tif/dot_general | solution.py:32
  326.3 18.3 %scatter_fusion.1 = f32[16,128,512]{2,1,0:T(8,128)} fusion(f32[16,128,512]{2,1,0:T(8,128)} %get-tuple-element.295, s32[32]{0:T(128)S(1)} %get-tuple-element.244, f32[32,128,512]{2,1,0:T(8,128)} %broadcast_multiply_fusion.6), kind=kCustom, calls=%fused_computation.3.clone.1 | custom fusion | flops 2097152 | bytes 25165952 | tf_op jit(solution)/shard_map/while/body/scatter-add | solution.py:35
  344.7 0.7 and_select_fusion.2
  345.4 0.1 compare_select_fusion.7
  345.5 2.8 gather_fusion.1
  348.2 7.3 %broadcast_multiply_fusion.6 = f32[32,128,512]{2,1,0:T(8,128)} fusion(f32[32]{0:T(128)S(1)} %and_select_fusion.2, bf16[32,128,512]{2,1,0:T(8,128)(2,1)} %gather_fusion.1, bf16[256,128,128]{2,1,0:T(8,128)(2,1)} %get-tuple-element.310, s32[]{:T(128)S(6)} %select_n.46), kind=kOutput, calls=%fused_computation.11.clone.1 | convolution fusion | flops 538968064 | bytes 13631620 | tf_op jit(solution)/shard_map/while/body/tji,tjf->tif/dot_general | solution.py:32
  355.5 18.5 %scatter_fusion.1 = f32[16,128,512]{2,1,0:T(8,128)} fusion(f32[16,128,512]{2,1,0:T(8,128)} %get-tuple-element.295, s32[32]{0:T(128)S(1)} %get-tuple-element.244, f32[32,128,512]{2,1,0:T(8,128)} %broadcast_multiply_fusion.6), kind=kCustom, calls=%fused_computation.3.clone.1 | custom fusion | flops 2097152 | bytes 25165952 | tf_op jit(solution)/shard_map/while/body/scatter-add | solution.py:35
  374.1 3.8 convert_element_type.37
  377.9 0.0 reduce-scatter.2.cloned.1.call-update
  377.9 2.0 fusion.14
  379.9 49.0 %all-reduce.3.cloned.1.call-done = f32[512,512]{1,0:T(8,128)} async-done(((f32[512,512]{1,0:T(8,128)}), f32[512,512]{1,0:T(8,128)}) %all-reduce.3.cloned.1.call-update) | async-done | bytes 1048592 | tf_op jit(solution)/shard_map/psum | solution.py:74
  428.9 2.3 broadcast_multiply_fusion.2
  431.2 173.9 %reduce-scatter.2.cloned.1.call-done = bf16[256,512]{1,0:T(8,128)(2,1)} async-done(((bf16[2048,512]{1,0:T(8,128)(2,1)}), bf16[256,512]{1,0:T(8,128)(2,1)}) %reduce-scatter.2.cloned.1.call-update) | async-done | bytes 262160 | tf_op jit(solution)/shard_map/reduce_scatter | solution.py:79
  (13 shorter events, 0.1 us)
Async XLA Ops:
  7.2 238.7 %copy-start = (bf16[512,512]{1,0:T(8,128)(2,1)S(1)}, bf16[512,512]{1,0:T(8,128)(2,1)}, u32[]{:S(2)}) copy-start(bf16[512,512]{1,0:T(8,128)(2,1)} %param.12) | copy-start | bytes 1572868
  7.2 55.1 %copy-start.1 = (s32[256]{0:T(256)S(1)}, s32[256]{0:T(256)}, u32[]{:S(2)}) copy-start(s32[256]{0:T(256)} %param.16) | copy-start | bytes 3076
  7.2 55.1 %copy-start.2 = (s32[256]{0:T(256)S(1)}, s32[256]{0:T(256)}, u32[]{:S(2)}) copy-start(s32[256]{0:T(256)} %param.15) | copy-start | bytes 3076
  7.2 54.8 %all-gather.3.cloned.1.call-start = ((), (), s32[]{:S(2)}) async-start(), calls=%async_computation.1 | async-start | bytes 2359296 | tf_op jit(solution)/shard_map/all_gather | solution.py:50
  7.9 237.9 %all-gather.5.cloned.1.call-start = ((), (), s32[]{:S(2)}) async-start(), calls=%async_computation.2 | async-start | bytes 1310720 | tf_op jit(solution)/shard_map/all_gather | solution.py:64
  8.7 420.2 %all-reduce.3.cloned.1.call-start = ((), (), s32[]{:S(2)}) async-start(), calls=%async_computation.3 | async-start | bytes 2097152 | tf_op jit(solution)/shard_map/psum | solution.py:74
  254.2 350.8 %reduce-scatter.2.cloned.1.call-start = ((), (), s32[]{:S(2)}) async-start(), calls=%async_computation.4 | async-start | bytes 2359296 | tf_op jit(solution)/shard_map/reduce_scatter | solution.py:79
Sparse Core Ops, SparseCore 0:
  10.1 51.7 all-gather.2
  63.5 15.2 all-gather.4
  254.3 174.4 all-reduce.2
  432.8 172.1 reduce-scatter.1
where the time goes:
time: 614 us; the launch traced here: 612 us
  waiting for transfers between devices  277 us (45%)
  other arithmetic  135 us (22%)
  blocking collectives  87.7 us (14%)
  matrix products  65.7 us (11%)
  local copies, waits for them, and re-layouts  31.2 us (5%)
  between operations  14.5 us (2%)
    reduce_scatter x1, waiting for transfers between devices, local(): lax.psum_scatter(contributions.reshape(-1, feature_width).astype(jnp.bflo...  174 us
    psum x1, blocking collectives, local(): aggregate_all = lax.psum(partial_value, 'rep').astype(jnp.bfloat16)  87.7 us
    scatter-add x4, other arithmetic, one_turn(): return totals.at[placed].add(product * (slot_mask * inside)[:, None, None])  73.9 us
    all_gather x1, waiting for transfers between devices, local(): gathered = lax.all_gather(features, 'node', axis=0, tiled=True)  52.6 us
    psum x1, waiting for transfers between devices, local(): weight_grad = lax.psum(weight_term, ('node', 'rep')) * scale  49 us
    scatter-add x4, other arithmetic, one_turn(): return totals.at[rows_here].add(product * slot_mask[:, None, None])  47.1 us
    dot_general x4, matrix products, one_turn(): jnp.einsum('tji,tjf->tif', values, sources[rows_here], preferred_element_...  29.1 us
    dot_general x4, matrix products, one_turn(): jnp.einsum('tij,tjf->tif', values, sources[cols_here], preferred_element_...  28.2 us
  transfers between devices with their start and end apart: 4, of which 3 were waited for; matrix products, arithmetic and copies ran while one was open for 37% of the time, Pallas kernels for 0%

commit v1 on v0

--- a/solution.py
+++ b/solution.py
@@ -60,7 +60,9 @@
         False,
         0,
     ).reshape(block_count * TB, feature_width)
-    aggregate_all = lax.psum(partial_value, "rep").astype(jnp.bfloat16)
+    aggregate_all = jnp.sum(lax.all_gather(partial_value, axis_name="rep"), axis=0).astype(
+        jnp.bfloat16
+    )
     cotangent_all = lax.all_gather(cotangent, "rep", axis=0, tiled=True)
     pre = jnp.dot(aggregate_all, weight, preferred_element_type=jnp.float32)
     activated, pullback = jax.vjp(smooth_gate, pre)

time: 614 us -> 649 us (1.057)
  waiting for transfers between devices: 277 us -> 395 us
  blocking collectives: 87.7 us -> 0 us
    all_gather x0 -> x1, waiting for transfers between devices: none -> 149 us  [local(): lax.all_gather(partial_value, axis_name='rep')]
    psum x1 -> x0, blocking collectives: 87.7 us -> none  [local(): aggregate_all = lax.psum(partial_value, 'rep').astype(jnp.bfloat16)]
    psum x1, waiting for transfers between devices: 49 us -> 5.2 us  [local(): weight_grad = lax.psum(weight_term, ('node', 'rep')) * scale]
    all_gather x1, waiting for transfers between devices: 0.01 us -> 13.7 us  [local(): cotangent_all = lax.all_gather(cotangent, 'rep', axis=0, tiled=True)]
  transfers between devices with their start and end apart: 4 -> 5, of which waited for: 3 -> 5; matrix products, arithmetic and copies ran while one was open for 37% -> 20% of each run, Pallas kernels for 0% -> 0%
where the time goes in v1:
time: 649 us; the launch traced here: 646 us
  waiting for transfers between devices  395 us (61%)
  other arithmetic  140 us (22%)
  matrix products  64.1 us (10%)
  local copies, waits for them, and re-layouts  32.7 us (5%)
  between operations  14.5 us (2%)
    reduce_scatter x1, waiting for transfers between devices, local(): lax.psum_scatter(contributions.reshape(-1, feature_width).astype(jnp.bflo...  172 us
    all_gather x1, waiting for transfers between devices, local(): lax.all_gather(partial_value, axis_name='rep')  149 us
    scatter-add x4, other arithmetic, one_turn(): return totals.at[placed].add(product * (slot_mask * inside)[:, None, None])  73.8 us
    all_gather x1, waiting for transfers between devices, local(): gathered = lax.all_gather(features, 'node', axis=0, tiled=True)  53.3 us
    scatter-add x4, other arithmetic, one_turn(): return totals.at[rows_here].add(product * slot_mask[:, None, None])  47.1 us
    dot_general x4, matrix products, one_turn(): jnp.einsum('tji,tjf->tif', values, sources[rows_here], preferred_element_...  29.1 us
    dot_general x4, matrix products, one_turn(): jnp.einsum('tij,tjf->tif', values, sources[cols_here], preferred_element_...  27.9 us
    gather x4, local copies, waits for them, and re-layouts, one_turn(): sources[cols_here]  17.5 us
  transfers between devices with their start and end apart: 5, of which 5 were waited for; matrix products, arithmetic and copies ran while one was open for 20% of the time, Pallas kernels for 0%

profile of v1, /device:TPU:0, one launch (start us, length us, event | category | flops | bytes accessed | tf_op | source)
XLA Modules:
  0.0 646.3 jit_solution(16538690188308362931)
XLA Ops:
  7.2 0.0 all-gather.4.cloned.1.call-start
  7.2 0.7 all-gather.4.cloned.1.call-update
  7.9 0.0 all-gather.6.cloned.1.call-start
  8.6 53.3 %all-gather.4.cloned.1.call-done = bf16[2048,512]{1,0:T(8,128)(2,1)} async-done(((bf16[256,512]{1,0:T(8,128)(2,1)}), bf16[2048,512]{1,0:T(8,128)(2,1)}) %all-gather.4.cloned.1.call-update) | async-done | bytes 2097168 | tf_op jit(solution)/shard_map/all_gather | solution.py:50
  62.0 0.2 broadcast_in_dim.20
  62.3 95.7 %while.20 = (s32[]{:T(128)}, f32[8,128,512]{2,1,0:T(8,128)S(1)}, s32[]{:T(128)}, s32[256]{0:T(256)S(1)}, bf16[256,128,128]{2,1,0:T(8,128)(2,1)}, /*index=5*/s32[...) while((s32[]{:T(128)}, f32[8,128,512]{2,1,0:T(8,128)S(1)}, ...), condition=%wide.region_2.3_spmd, body=%wide.region_0.2_spmd.sunk | while | flops 541066560 | bytes 47191344 | solution.py:41
  62.3 0.7 compare_convert_fusion.3
  62.9 0.1 compare_select_fusion.6
  63.0 4.4 gather_fusion
  67.4 7.0 %broadcast_multiply_fusion.5 = f32[32,128,512]{2,1,0:T(8,128)} fusion(f32[32]{0:T(128)S(1)} %compare_convert_fusion.3, bf16[32,128,512]{2,1,0:T(8,128)(2,1)} %gather_fusion, bf16[256,128,128]{2,1,0:T(8,128)(2,1)} %get-tuple-element.282, s32[]{:T(128)S(6)} %select_n.44), kind=kOutput, calls=%fused_computation.4.clone.1 | convolution fusion | flops 538968064 | bytes 13631620 | tf_op jit(solution)/shard_map/while/body/tij,tjf->tif/dot_general | solution.py:36
  74.4 11.7 %scatter_fusion = f32[8,128,512]{2,1,0:T(8,128)S(1)} fusion(f32[8,128,512]{2,1,0:T(8,128)S(1)} %get-tuple-element.267, s32[32]{0:T(128)S(1)} %get-tuple-element.242, f32[32,128,512]{2,1,0:T(8,128)} %broadcast_multiply_fusion.5), kind=kCustom, calls=%fused_computation.2.clone.1 | custom fusion | flops 2097152 | bytes 25165952 | tf_op jit(solution)/shard_map/while/body/scatter-add | solution.py:39
  86.2 0.7 compare_convert_fusion.3
  86.8 0.1 compare_select_fusion.6
  86.9 4.4 gather_fusion
  91.3 7.0 %broadcast_multiply_fusion.5 = f32[32,128,512]{2,1,0:T(8,128)} fusion(f32[32]{0:T(128)S(1)} %compare_convert_fusion.3, bf16[32,128,512]{2,1,0:T(8,128)(2,1)} %gather_fusion, bf16[256,128,128]{2,1,0:T(8,128)(2,1)} %get-tuple-element.282, s32[]{:T(128)S(6)} %select_n.44), kind=kOutput, calls=%fused_computation.4.clone.1 | convolution fusion | flops 538968064 | bytes 13631620 | tf_op jit(solution)/shard_map/while/body/tij,tjf->tif/dot_general | solution.py:36
  98.3 11.8 %scatter_fusion = f32[8,128,512]{2,1,0:T(8,128)S(1)} fusion(f32[8,128,512]{2,1,0:T(8,128)S(1)} %get-tuple-element.267, s32[32]{0:T(128)S(1)} %get-tuple-element.242, f32[32,128,512]{2,1,0:T(8,128)} %broadcast_multiply_fusion.5), kind=kCustom, calls=%fused_computation.2.clone.1 | custom fusion | flops 2097152 | bytes 25165952 | tf_op jit(solution)/shard_map/while/body/scatter-add | solution.py:39
  110.1 0.7 compare_convert_fusion.3
  110.7 0.1 compare_select_fusion.6
  110.8 4.4 gather_fusion
  115.2 7.0 %broadcast_multiply_fusion.5 = f32[32,128,512]{2,1,0:T(8,128)} fusion(f32[32]{0:T(128)S(1)} %compare_convert_fusion.3, bf16[32,128,512]{2,1,0:T(8,128)(2,1)} %gather_fusion, bf16[256,128,128]{2,1,0:T(8,128)(2,1)} %get-tuple-element.282, s32[]{:T(128)S(6)} %select_n.44), kind=kOutput, calls=%fused_computation.4.clone.1 | convolution fusion | flops 538968064 | bytes 13631620 | tf_op jit(solution)/shard_map/while/body/tij,tjf->tif/dot_general | solution.py:36
  122.2 11.7 %scatter_fusion = f32[8,128,512]{2,1,0:T(8,128)S(1)} fusion(f32[8,128,512]{2,1,0:T(8,128)S(1)} %get-tuple-element.267, s32[32]{0:T(128)S(1)} %get-tuple-element.242, f32[32,128,512]{2,1,0:T(8,128)} %broadcast_multiply_fusion.5), kind=kCustom, calls=%fused_computation.2.clone.1 | custom fusion | flops 2097152 | bytes 25165952 | tf_op jit(solution)/shard_map/while/body/scatter-add | solution.py:39
  134.0 0.7 compare_convert_fusion.3
  134.6 0.1 compare_select_fusion.6
  134.7 4.4 gather_fusion
  139.1 7.0 %broadcast_multiply_fusion.5 = f32[32,128,512]{2,1,0:T(8,128)} fusion(f32[32]{0:T(128)S(1)} %compare_convert_fusion.3, bf16[32,128,512]{2,1,0:T(8,128)(2,1)} %gather_fusion, bf16[256,128,128]{2,1,0:T(8,128)(2,1)} %get-tuple-element.282, s32[]{:T(128)S(6)} %select_n.44), kind=kOutput, calls=%fused_computation.4.clone.1 | convolution fusion | flops 538968064 | bytes 13631620 | tf_op jit(solution)/shard_map/while/body/tij,tjf->tif/dot_general | solution.py:36
  146.1 11.8 %scatter_fusion = f32[8,128,512]{2,1,0:T(8,128)S(1)} fusion(f32[8,128,512]{2,1,0:T(8,128)S(1)} %get-tuple-element.267, s32[32]{0:T(128)S(1)} %get-tuple-element.242, f32[32,128,512]{2,1,0:T(8,128)} %broadcast_multiply_fusion.5), kind=kCustom, calls=%fused_computation.2.clone.1 | custom fusion | flops 2097152 | bytes 25165952 | tf_op jit(solution)/shard_map/while/body/scatter-add | solution.py:39
  157.9 1.4 copy-done.1
  159.3 0.0 all-gather.8.cloned.1.call-start
  159.4 0.7 all-gather.8.cloned.1.call-update
  160.0 0.0 all-reduce.2.cloned.1.call-start
  160.1 148.7 %all-gather.6.cloned.1.call-done = f32[4,1024,512]{2,1,0:T(8,128)} async-done(((f32[1,1024,512]{2,1,0:T(8,128)}), f32[4,1024,512]{2,1,0:T(8,128)}) %all-gather.6.cloned.1.call-update) | async-done | bytes 8388624 | tf_op jit(solution)/shard_map/all_gather | solution.py:63
  308.8 4.6 reduce_sum.9
  313.4 13.7 %all-gather.8.cloned.1.call-done = bf16[1024,512]{1,0:T(8,128)(2,1)} async-done(((bf16[256,512]{1,0:T(8,128)(2,1)}), bf16[1024,512]{1,0:T(8,128)(2,1)}) %all-gather.8.cloned.1.call-update) | async-done | bytes 1048592 | tf_op jit(solution)/shard_map/all_gather | solution.py:66
  327.1 5.0 fusion.6
  332.1 0.7 convolution_convert_fusion
  332.9 1.3 fusion.15
  334.2 0.0 reduce-scatter.2.cloned.1.call-start
  334.2 2.5 broadcast_in_dim.21
  336.7 117.2 %while.21 = (s32[]{:T(128)}, f32[16,128,512]{2,1,0:T(8,128)}, s32[]{:T(128)}, s32[256]{0:T(256)S(1)}, bf16[256,128,128]{2,1,0:T(8,128)(2,1)}, /*index=5*/s32[256...) while((s32[]{:T(128)}, f32[16,128,512]{2,1,0:T(8,128)}, ...), condition=%wide.region_7.8_spmd, body=%wide.region_5.7_spmd.sunk | while | flops 541066688 | bytes 47191480 | solution.py:41
  336.7 0.7 and_select_fusion.2
  337.4 0.1 compare_select_fusion.7
  337.5 2.8 gather_fusion.1
  340.3 7.3 %broadcast_multiply_fusion.6 = f32[32,128,512]{2,1,0:T(8,128)} fusion(f32[32]{0:T(128)S(1)} %and_select_fusion.2, bf16[32,128,512]{2,1,0:T(8,128)(2,1)} %gather_fusion.1, bf16[256,128,128]{2,1,0:T(8,128)(2,1)} %get-tuple-element.318, s32[]{:T(128)S(6)} %select_n.46), kind=kOutput, calls=%fused_computation.11.clone.1 | convolution fusion | flops 538968064 | bytes 13631620 | tf_op jit(solution)/shard_map/while/body/tji,tjf->tif/dot_general | solution.py:32
  347.6 18.5 %scatter_fusion.1 = f32[16,128,512]{2,1,0:T(8,128)} fusion(f32[16,128,512]{2,1,0:T(8,128)} %get-tuple-element.303, s32[32]{0:T(128)S(1)} %get-tuple-element.252, f32[32,128,512]{2,1,0:T(8,128)} %broadcast_multiply_fusion.6), kind=kCustom, calls=%fused_computation.3.clone.1 | custom fusion | flops 2097152 | bytes 25165952 | tf_op jit(solution)/shard_map/while/body/scatter-add | solution.py:35
  366.0 0.7 and_select_fusion.2
  366.8 0.1 compare_select_fusion.7
  366.8 2.8 gather_fusion.1
  369.6 7.3 %broadcast_multiply_fusion.6 = f32[32,128,512]{2,1,0:T(8,128)} fusion(f32[32]{0:T(128)S(1)} %and_select_fusion.2, bf16[32,128,512]{2,1,0:T(8,128)(2,1)} %gather_fusion.1, bf16[256,128,128]{2,1,0:T(8,128)(2,1)} %get-tuple-element.318, s32[]{:T(128)S(6)} %select_n.46), kind=kOutput, calls=%fused_computation.11.clone.1 | convolution fusion | flops 538968064 | bytes 13631620 | tf_op jit(solution)/shard_map/while/body/tji,tjf->tif/dot_general | solution.py:32
  376.9 18.5 %scatter_fusion.1 = f32[16,128,512]{2,1,0:T(8,128)} fusion(f32[16,128,512]{2,1,0:T(8,128)} %get-tuple-element.303, s32[32]{0:T(128)S(1)} %get-tuple-element.252, f32[32,128,512]{2,1,0:T(8,128)} %broadcast_multiply_fusion.6), kind=kCustom, calls=%fused_computation.3.clone.1 | custom fusion | flops 2097152 | bytes 25165952 | tf_op jit(solution)/shard_map/while/body/scatter-add | solution.py:35
  395.4 0.7 and_select_fusion.2
  396.2 0.1 compare_select_fusion.7
  396.2 2.8 gather_fusion.1
  399.0 7.3 %broadcast_multiply_fusion.6 = f32[32,128,512]{2,1,0:T(8,128)} fusion(f32[32]{0:T(128)S(1)} %and_select_fusion.2, bf16[32,128,512]{2,1,0:T(8,128)(2,1)} %gather_fusion.1, bf16[256,128,128]{2,1,0:T(8,128)(2,1)} %get-tuple-element.318, s32[]{:T(128)S(6)} %select_n.46), kind=kOutput, calls=%fused_computation.11.clone.1 | convolution fusion | flops 538968064 | bytes 13631620 | tf_op jit(solution)/shard_map/while/body/tji,tjf->tif/dot_general | solution.py:32
  406.3 18.3 %scatter_fusion.1 = f32[16,128,512]{2,1,0:T(8,128)} fusion(f32[16,128,512]{2,1,0:T(8,128)} %get-tuple-element.303, s32[32]{0:T(128)S(1)} %get-tuple-element.252, f32[32,128,512]{2,1,0:T(8,128)} %broadcast_multiply_fusion.6), kind=kCustom, calls=%fused_computation.3.clone.1 | custom fusion | flops 2097152 | bytes 25165952 | tf_op jit(solution)/shard_map/while/body/scatter-add | solution.py:35
  424.6 0.7 and_select_fusion.2
  425.3 0.1 compare_select_fusion.7
  425.4 2.8 gather_fusion.1
  428.1 7.3 %broadcast_multiply_fusion.6 = f32[32,128,512]{2,1,0:T(8,128)} fusion(f32[32]{0:T(128)S(1)} %and_select_fusion.2, bf16[32,128,512]{2,1,0:T(8,128)(2,1)} %gather_fusion.1, bf16[256,128,128]{2,1,0:T(8,128)(2,1)} %get-tuple-element.318, s32[]{:T(128)S(6)} %select_n.46), kind=kOutput, calls=%fused_computation.11.clone.1 | convolution fusion | flops 538968064 | bytes 13631620 | tf_op jit(solution)/shard_map/while/body/tji,tjf->tif/dot_general | solution.py:32
  435.4 18.5 %scatter_fusion.1 = f32[16,128,512]{2,1,0:T(8,128)} fusion(f32[16,128,512]{2,1,0:T(8,128)} %get-tuple-element.303, s32[32]{0:T(128)S(1)} %get-tuple-element.252, f32[32,128,512]{2,1,0:T(8,128)} %broadcast_multiply_fusion.6), kind=kCustom, calls=%fused_computation.3.clone.1 | custom fusion | flops 2097152 | bytes 25165952 | tf_op jit(solution)/shard_map/while/body/scatter-add | solution.py:35
  453.9 3.8 convert_element_type.37
  457.8 2.0 fusion.14
  459.8 5.2 all-reduce.2.cloned.1.call-done
  465.0 2.3 broadcast_multiply_fusion.2
  467.3 172.5 %reduce-scatter.2.cloned.1.call-done = bf16[256,512]{1,0:T(8,128)(2,1)} async-done(((bf16[2048,512]{1,0:T(8,128)(2,1)}), bf16[256,512]{1,0:T(8,128)(2,1)}) %reduce-scatter.2.cloned.1.call-update) | async-done | bytes 262160 | tf_op jit(solution)/shard_map/reduce_scatter | solution.py:81
  (18 shorter events, 0.1 us)
Async XLA Ops:
  7.2 319.9 %copy-start = (bf16[512,512]{1,0:T(8,128)(2,1)S(1)}, bf16[512,512]{1,0:T(8,128)(2,1)}, u32[]{:S(2)}) copy-start(bf16[512,512]{1,0:T(8,128)(2,1)} %param.12) | copy-start | bytes 1572868
  7.2 55.1 %copy-start.2 = (s32[256]{0:T(256)S(1)}, s32[256]{0:T(256)}, u32[]{:S(2)}) copy-start(s32[256]{0:T(256)} %param.16) | copy-start | bytes 3076
  7.2 55.1 %copy-start.3 = (s32[256]{0:T(256)S(1)}, s32[256]{0:T(256)}, u32[]{:S(2)}) copy-start(s32[256]{0:T(256)} %param.15) | copy-start | bytes 3076
  7.2 54.8 %all-gather.4.cloned.1.call-start = ((), (), s32[]{:S(2)}) async-start(), calls=%async_computation.1 | async-start | bytes 2359296 | tf_op jit(solution)/shard_map/all_gather | solution.py:50
  7.9 300.9 %all-gather.6.cloned.1.call-start = ((), (), s32[]{:S(2)}) async-start(), calls=%async_computation.2 | async-start | bytes 10485760 | tf_op jit(solution)/shard_map/all_gather | solution.py:63
  157.9 1.4 copy-start.1
  159.3 167.8 %all-gather.8.cloned.1.call-start = ((), (), s32[]{:S(2)}) async-start(), calls=%async_computation.3 | async-start | bytes 1310720 | tf_op jit(solution)/shard_map/all_gather | solution.py:66
  160.0 304.9 %all-reduce.2.cloned.1.call-start = ((), (), s32[]{:S(2)}) async-start(), calls=%async_computation.4 | async-start | bytes 2097152 | tf_op jit(solution)/shard_map/psum | solution.py:76
  334.2 305.6 %reduce-scatter.2.cloned.1.call-start = ((), (), s32[]{:S(2)}) async-start(), calls=%async_computation.5 | async-start | bytes 2359296 | tf_op jit(solution)/shard_map/reduce_scatter | solution.py:81
Sparse Core Ops, SparseCore 0:
  10.1 51.7 all-gather.3
  159.4 149.3 all-gather.5
  310.4 16.6 all-gather.7
  334.3 130.6 all-reduce.1
  468.9 170.8 reduce-scatter.1
